TPU v7x, 256 devices: a whole 4x4x8 slice. The times are simulated.
256 devices in a mesh: row: 16 (over z, core), col: 16 (over x, y).
Axes of the slice: x: 4, y: 4, z: 8, core: 2. Of those that a mesh axis runs over, the one named last changes fastest.
Arguments:
- tensor: float32 [12, 8192, 8192], P(None, 'row', 'col'), may hold values from -6 to 6
- factor_b: float32 [8192, 128], P(('col', 'row')), may hold values from -0.0625 to 0.0625
- factor_c: float32 [12, 128], replicated, may hold values from -1.75 to 1.75
Outputs:
- a_update: float32 [8192, 128], P(('row', 'col'))
- b_update: float32 [8192, 128], P(('col', 'row'))
All inputs are finite; a program needn't handle non-finite values.
Results may differ from a plain program's by a relative error of at most 0.00012.
Values sent between devices are 32-bit elements; how exact they have to be, the bound alone decides.
No kernel may reach another device: no remote copies, remote signals or barrier semaphores. Data moves between devices by JAX's collectives and lax.ppermute only.
A program may use at most 64 MiB of HBM per device.

v0:
```python
import jax
import jax.numpy as jnp
from jax import lax
from jax.sharding import PartitionSpec as P

EPSILON = 1e-06


def solve_system(rhs, system):
    highest = lax.Precision.HIGHEST
    lower = jnp.linalg.cholesky(system)
    inverse = jax.scipy.linalg.cho_solve(
        (lower, True), jnp.eye(system.shape[0], dtype=system.dtype)
    )
    return jnp.dot(rhs, inverse, precision=highest)


def gram_of(matrix):
    return jnp.dot(matrix.T, matrix, precision=lax.Precision.HIGHEST)


def per_device(tensor, factor_b, factor_c):
    highest = lax.Precision.HIGHEST
    rows_block = tensor.shape[1]
    cols_block = tensor.shape[2]
    rank_width = factor_c.shape[1]
    owned_a = rows_block // lax.axis_size("col")
    owned_b = cols_block // lax.axis_size("row")
    c_gram = gram_of(factor_c)
    empty_b = jnp.zeros((cols_block, rank_width), jnp.float32)
    gram_b = lax.psum(gram_of(factor_b), ("row", "col"))
    block = tensor
    khatri = factor_c[:, None, :] * lax.all_gather(factor_b, "row", axis=0, tiled=True)[None, :, :]
    partial_a = jnp.einsum("kij,kjr->ir", block, khatri, precision=highest)
    whole_a = lax.psum(partial_a, "col")
    summed_a = lax.dynamic_slice_in_dim(whole_a, lax.axis_index("col") * owned_a, owned_a, 0)
    a_update = solve_system(summed_a, c_gram * gram_b)
    squares = lax.psum(jnp.sum(a_update * a_update, axis=0), ("row", "col"))
    factor_a = a_update / jnp.sqrt(squares + EPSILON)
    gram_a = lax.psum(gram_of(factor_a), ("row", "col"))
    block = tensor
    khatri = factor_c[:, None, :] * lax.all_gather(factor_a, "col", axis=0, tiled=True)[None, :, :]
    partial_b = empty_b + jnp.einsum("kij,kir->jr", block, khatri, precision=highest)
    whole_b = lax.psum(partial_b, "row")
    summed_b = lax.dynamic_slice_in_dim(whole_b, lax.axis_index("row") * owned_b, owned_b, 0)
    b_update = solve_system(summed_b, c_gram * gram_a)
    return (a_update, b_update)


def solution(mesh):
    placed = (P(None, "row", "col"), P(("col", "row"), None), P())
    return jax.shard_map(
        per_device,
        mesh=mesh,
        in_specs=placed,
        out_specs=(P(("row", "col"), None), P(("col", "row"), None)),
        check_vma=False,
    )
```

profile of v0, /device:TPU:1, one launch (start us, length us, event | category | flops | bytes accessed | tf_op | source)
XLA Modules:
  0.0 809.7 jit_solution(5450451104905007428)
XLA Ops:
  7.2 1.7 fusion.35
  9.0 22.3 %all_gather.6 = f32[512,128]{1,0:T(8,128)S(1)} all-gather(f32[32,128]{1,0:T(8,128)} %param.7), channel_id=1, replica_groups=mesh['row'=16,'col'=16] {'row'}, dimensions={0}, use_global_device_ids=true | all-gather | bytes 278528 | tf_op jit(solution)/shard_map/all_gather | solution.py:33
  31.2 18.3 %fusion.8 = f32[512,128]{0,1:T(8,128)} fusion(f32[12,512,512]{2,1,0:T(8,128)} %param.6, f32[512,128]{1,0:T(8,128)S(1)} %all_gather.6, f32[12,128]{1,0:T(8,128)} %param.8), kind=kOutput, calls=%fused_computation.8 | convolution fusion | flops 4832624640 | bytes 13113344 | tf_op jit(solution)/shard_map/kij,kjr->ir/dot_general | solution.py:34
  49.8 209.2 %all-reduce.7.cloned.1.call-done = f32[128,128]{0,1:T(8,128)} async-done(((f32[128,128]{0,1:T(8,128)}), f32[128,128]{0,1:T(8,128)}) %all-reduce.7.cloned.1.call-update) | async-done | bytes 65552 | tf_op jit(solution)/shard_map/psum | solution.py:31
  259.1 1.1 fusion.34
  260.3 11.7 %cholesky.44 = f32[128,128]{1,0:T(8,128)S(1)} custom-call(f32[128,128]{1,0:T(8,128)S(1)} %fusion.27), custom_call_target="Cholesky" | custom-call | tf_op jit(solution)/shard_map/jit(cholesky)/cholesky | solution.py:11
  272.1 0.6 compare_reduce_fusion.1
  272.7 0.7 fusion.18
  273.4 9.8 %custom-call.8 = f32[1,128,128]{1,2,0:T(8,128)S(1)} custom-call(f32[1,128,128]{2,1,0:T(8,128)S(1)} %fusion.18), custom_call_target="InvertDiagBlocksLowerTriangular" | custom-call | tf_op jit(solution)/shard_map/jit(_cho_solve)/triangular_solve | solution.py:12
  283.2 0.3 fusion.16
  283.7 68.0 %all-reduce.5.cloned.1.call-done = f32[512,128]{0,1:T(8,128)} async-done(((f32[512,128]{0,1:T(8,128)}), f32[512,128]{0,1:T(8,128)}) %all-reduce.5.cloned.1.call-update) | async-done | bytes 262160 | tf_op jit(solution)/shard_map/psum | solution.py:35
  351.7 1.2 multiply_reduce_fusion
  352.8 77.5 %psum.37 = f32[128]{0:T(128)S(1)} all-reduce(f32[128]{0:T(128)S(1)} %get-tuple-element.6), channel_id=1, replica_groups=mesh['row'=16,'col'=16] {'row','col'}, use_global_device_ids=true, to_apply=%region_5.0 | all-reduce | flops 128 | bytes 1024 | tf_op jit(solution)/shard_map/psum | solution.py:38
  430.3 0.9 fusion.36
  431.3 15.8 %all_gather.7 = f32[512,128]{1,0:T(8,128)S(1)} all-gather(f32[32,128]{1,0:T(8,128)S(1)} %broadcast_divide_fusion), channel_id=1, replica_groups=mesh['row'=16,'col'=16] {'col'}, dimensions={0}, use_global_device_ids=true | all-gather | bytes 278528 | tf_op jit(solution)/shard_map/all_gather | solution.py:42
  447.3 11.4 %fusion.11 = f32[512,128]{0,1:T(8,128)} fusion(f32[12,512,512]{2,1,0:T(8,128)} %param.6, f32[512,128]{1,0:T(8,128)S(1)} %all_gather.7, f32[12,128]{1,0:T(8,128)S(1)} %copy-done), kind=kOutput, calls=%fused_computation.9 | convolution fusion | flops 4832624640 | bytes 13113344 | tf_op jit(solution)/shard_map/kij,kir->jr/dot_general | solution.py:43
  458.8 234.0 %all-reduce.11.cloned.1.call-done = f32[128,128]{0,1:T(8,128)} async-done(((f32[128,128]{0,1:T(8,128)}), f32[128,128]{0,1:T(8,128)}) %all-reduce.11.cloned.1.call-update) | async-done | bytes 65552 | tf_op jit(solution)/shard_map/psum | solution.py:40
  692.8 0.9 mul.48
  693.8 11.7 %cholesky.55 = f32[128,128]{1,0:T(8,128)S(1)} custom-call(f32[128,128]{1,0:T(8,128)S(1)} %fusion.23), custom_call_target="Cholesky" | custom-call | tf_op jit(solution)/shard_map/jit(cholesky)/cholesky | solution.py:11
  705.5 0.6 compare_reduce_fusion
  706.2 0.7 fusion.19
  706.8 9.8 %custom-call.9 = f32[1,128,128]{1,2,0:T(8,128)S(1)} custom-call(f32[1,128,128]{2,1,0:T(8,128)S(1)} %fusion.19), custom_call_target="InvertDiagBlocksLowerTriangular" | custom-call | tf_op jit(solution)/shard_map/jit(_cho_solve)/triangular_solve | solution.py:12
  717.2 84.3 %all-reduce.9.cloned.1.call-done = f32[512,128]{0,1:T(8,128)} async-done(((f32[512,128]{0,1:T(8,128)}), f32[512,128]{0,1:T(8,128)}) %all-reduce.9.cloned.1.call-update) | async-done | bytes 262160 | tf_op jit(solution)/shard_map/psum | solution.py:44
  801.4 1.8 fusion.28
  (23 shorter events, 1.6 us)
Async XLA Ops:
  7.2 251.9 %all-reduce.7.cloned.1.call-start = ((), (), s32[]{:S(2)}) async-start(), calls=%async_computation.1 | async-start | bytes 131072 | tf_op jit(solution)/shard_map/psum | solution.py:31
  8.9 342.7 %all-reduce.5.cloned.1.call-start = ((), (), s32[]{:S(2)}) async-start(), calls=%async_computation | async-start | bytes 524288 | tf_op jit(solution)/shard_map/psum | solution.py:35
  31.2 227.8 %copy-start = (f32[12,128]{1,0:T(8,128)S(1)}, f32[12,128]{1,0:T(8,128)}, u32[]{:S(2)}) copy-start(f32[12,128]{1,0:T(8,128)} %param.8) | copy-start | bytes 18436
  49.6 643.2 %all-reduce.11.cloned.1.call-start = ((), (), s32[]{:S(2)}) async-start(), calls=%async_computation.3 | async-start | bytes 131072 | tf_op jit(solution)/shard_map/psum | solution.py:40
  352.8 105.9 %copy-start.1 = (f32[32,128]{1,0:T(8,128)}, f32[32,128]{1,0:T(8,128)S(1)}, u32[]{:S(2)}) copy-start(f32[32,128]{1,0:T(8,128)S(1)} %get-tuple-element.7) | copy-start | bytes 49156
  447.1 354.4 %all-reduce.9.cloned.1.call-start = ((), (), s32[]{:S(2)}) async-start(), calls=%async_computation.2 | async-start | bytes 524288 | tf_op jit(solution)/shard_map/psum | solution.py:44
Sparse Core Ops, SparseCore 0:
  13.5 245.5 all-reduce.6
  262.2 89.3 all-reduce.4
  447.2 245.5 all-reduce.10
  695.0 106.4 all-reduce.8
where the time goes:
time: 810 us
  waiting for transfers between devices  596 us (74%)
  blocking collectives  116 us (14%)
  other arithmetic  46.6 us (6%)
  matrix products  37.4 us (5%)
  between operations  13.9 us (2%)
    psum x1, waiting for transfers between devices, per_device(): gram_a = lax.psum(gram_of(factor_a), ('row', 'col'))  234 us
    psum x1, waiting for transfers between devices, per_device(): gram_b = lax.psum(gram_of(factor_b), ('row', 'col'))  209 us
    psum x1, waiting for transfers between devices, per_device(): whole_b = lax.psum(partial_b, 'row')  84.3 us
    psum x1, blocking collectives, per_device(): squares = lax.psum(jnp.sum(a_update * a_update, axis=0), ('row', 'col'))  77.5 us
    psum x1, waiting for transfers between devices, per_device(): whole_a = lax.psum(partial_a, 'col')  68 us
    another operation x6, other arithmetic, solve_system(): lower = jnp.linalg.cholesky(system)  24.8 us
    all_gather x1, blocking collectives, per_device(): lax.all_gather(factor_b, 'row', axis=0, tiled=True)[None, :, :]  22.3 us
    another operation x4, other arithmetic, solve_system(): jax.scipy.linalg.cho_solve((lower, True), jnp.eye(system.shape[0], dtype=...  20.9 us
  transfers between devices with their start and end apart: 4, of which 4 were waited for; matrix products, arithmetic and copies ran while one was open for 10% of the time, Pallas kernels for 0%

commit v1 on v0

--- a/solution.py
+++ b/solution.py
@@ -32,7 +32,9 @@
     block = tensor
     khatri = factor_c[:, None, :] * lax.all_gather(factor_b, "row", axis=0, tiled=True)[None, :, :]
     partial_a = jnp.einsum("kij,kjr->ir", block, khatri, precision=highest)
-    whole_a = lax.psum(partial_a, "col")
+    whole_a = partial_a
+    for hop in (1, 2, 4, 8):
+        whole_a = whole_a + lax.ppermute(whole_a, "col", [(dev, dev ^ hop) for dev in range(16)])
     summed_a = lax.dynamic_slice_in_dim(whole_a, lax.axis_index("col") * owned_a, owned_a, 0)
     a_update = solve_system(summed_a, c_gram * gram_b)
     squares = lax.psum(jnp.sum(a_update * a_update, axis=0), ("row", "col"))

time: 810 us -> 748 us (0.923)
  waiting for transfers between devices: 596 us -> 534 us
    psum x1 -> x0, waiting for transfers between devices: 68 us -> none  [per_device(): whole_a = lax.psum(partial_a, 'col')]
  transfers between devices with their start and end apart: 4 -> 7, of which waited for: 4 -> 4; matrix products, arithmetic and copies ran while one was open for 10% -> 10% of each run, Pallas kernels for 0% -> 0%
where the time goes in v1:
time: 748 us; the launch traced here: 747 us
  waiting for transfers between devices  534 us (71%)
  blocking collectives  113 us (15%)
  other arithmetic  46.7 us (6%)
  matrix products  32.7 us (4%)
  between operations  13.9 us (2%)
    psum x1, waiting for transfers between devices, per_device(): gram_a = lax.psum(gram_of(factor_a), ('row', 'col'))  232 us
    psum x1, waiting for transfers between devices, per_device(): gram_b = lax.psum(gram_of(factor_b), ('row', 'col'))  211 us
    psum x1, waiting for transfers between devices, per_device(): whole_b = lax.psum(partial_b, 'row')  84.3 us
    psum x1, blocking collectives, per_device(): squares = lax.psum(jnp.sum(a_update * a_update, axis=0), ('row', 'col'))  73.8 us
    another operation x6, other arithmetic, solve_system(): lower = jnp.linalg.cholesky(system)  24.8 us
    all_gather x1, blocking collectives, per_device(): lax.all_gather(factor_b, 'row', axis=0, tiled=True)[None, :, :]  22.3 us
    another operation x4, other arithmetic, solve_system(): jax.scipy.linalg.cho_solve((lower, True), jnp.eye(system.shape[0], dtype=...  20.9 us
    all_gather x1, blocking collectives, per_device(): lax.all_gather(factor_a, 'col', axis=0, tiled=True)[None, :, :]  16.8 us
  transfers between devices with their start and end apart: 7, of which 4 were waited for; matrix products, arithmetic and copies ran while one was open for 10% of the time, Pallas kernels for 0%

profile of v1, /device:TPU:1, one launch (start us, length us, event | category | flops | bytes accessed | tf_op | source)
XLA Modules:
  0.0 747.5 jit_solution(16980393074663116779)
XLA Ops:
  7.2 1.7 fusion.35
  9.0 22.3 %all_gather.6 = f32[512,128]{1,0:T(8,128)S(1)} all-gather(f32[32,128]{1,0:T(8,128)} %param.7), channel_id=1, replica_groups=mesh['row'=16,'col'=16] {'row'}, dimensions={0}, use_global_device_ids=true | all-gather | bytes 278528 | tf_op jit(solution)/shard_map/all_gather | solution.py:33
  31.4 15.5 %fusion.8 = f32[512,128]{0,1:T(8,128)S(1)} fusion(f32[12,512,512]{2,1,0:T(8,128)} %param.6, f32[512,128]{0,1:T(8,128)S(1)} %copy.5, f32[12,128]{1,0:T(8,128)} %param.8), kind=kOutput, calls=%fused_computation.8 | convolution fusion | flops 4832624640 | bytes 13113344 | tf_op jit(solution)/shard_map/kij,kjr->ir/dot_general | solution.py:34
  46.9 1.4 collective-permute-start
  48.3 210.7 %all-reduce.4.cloned.1.call-done = f32[128,128]{0,1:T(8,128)} async-done(((f32[128,128]{0,1:T(8,128)}), f32[128,128]{0,1:T(8,128)}) %all-reduce.4.cloned.1.call-update) | async-done | bytes 65552 | tf_op jit(solution)/shard_map/psum | solution.py:31
  259.0 1.1 fusion.34
  260.3 1.7 collective-permute-start.1
  262.0 11.7 %cholesky.44 = f32[128,128]{1,0:T(8,128)S(1)} custom-call(f32[128,128]{1,0:T(8,128)S(1)} %fusion.29), custom_call_target="Cholesky" | custom-call | tf_op jit(solution)/shard_map/jit(cholesky)/cholesky | solution.py:11
  273.8 1.8 collective-permute-start.2
  276.2 0.7 fusion.18
  276.9 9.8 %custom-call.8 = f32[1,128,128]{1,2,0:T(8,128)S(1)} custom-call(f32[1,128,128]{2,1,0:T(8,128)S(1)} %fusion.18), custom_call_target="InvertDiagBlocksLowerTriangular" | custom-call | tf_op jit(solution)/shard_map/jit(_cho_solve)/triangular_solve | solution.py:12
  286.7 2.3 collective-permute-start.3
  289.6 6.5 collective-permute-done.3
  296.4 73.8 %psum.29 = f32[128]{0:T(128)S(1)} all-reduce(f32[128]{0:T(128)S(1)} %get-tuple-element.6), channel_id=1, replica_groups=mesh['row'=16,'col'=16] {'row','col'}, use_global_device_ids=true, to_apply=%region_4.0 | all-reduce | flops 128 | bytes 1024 | tf_op jit(solution)/shard_map/psum | solution.py:40
  370.2 0.9 fusion.36
  371.1 16.8 %all_gather.7 = f32[512,128]{1,0:T(8,128)S(1)} all-gather(f32[32,128]{1,0:T(8,128)S(1)} %broadcast_divide_fusion), channel_id=1, replica_groups=mesh['row'=16,'col'=16] {'col'}, dimensions={0}, use_global_device_ids=true | all-gather | bytes 278528 | tf_op jit(solution)/shard_map/all_gather | solution.py:44
  388.1 10.4 %fusion.11 = f32[512,128]{0,1:T(8,128)} fusion(f32[12,512,512]{2,1,0:T(8,128)} %param.6, f32[512,128]{0,1:T(8,128)S(1)} %copy.9, f32[12,128]{1,0:T(8,128)S(1)} %copy-done), kind=kOutput, calls=%fused_computation.9 | convolution fusion | flops 4832624640 | bytes 13113344 | tf_op jit(solution)/shard_map/kij,kir->jr/dot_general | solution.py:45
  398.5 232.0 %all-reduce.8.cloned.1.call-done = f32[128,128]{0,1:T(8,128)} async-done(((f32[128,128]{0,1:T(8,128)}), f32[128,128]{0,1:T(8,128)}) %all-reduce.8.cloned.1.call-update) | async-done | bytes 65552 | tf_op jit(solution)/shard_map/psum | solution.py:42
  630.6 0.9 mul.48
  631.5 11.7 %cholesky.55 = f32[128,128]{1,0:T(8,128)S(1)} custom-call(f32[128,128]{1,0:T(8,128)S(1)} %fusion.25), custom_call_target="Cholesky" | custom-call | tf_op jit(solution)/shard_map/jit(cholesky)/cholesky | solution.py:11
  643.9 0.7 fusion.19
  644.6 9.8 %custom-call.9 = f32[1,128,128]{1,2,0:T(8,128)S(1)} custom-call(f32[1,128,128]{2,1,0:T(8,128)S(1)} %fusion.19), custom_call_target="InvertDiagBlocksLowerTriangular" | custom-call | tf_op jit(solution)/shard_map/jit(_cho_solve)/triangular_solve | solution.py:12
  654.9 84.3 %all-reduce.6.cloned.1.call-done = f32[512,128]{0,1:T(8,128)} async-done(((f32[512,128]{0,1:T(8,128)}), f32[512,128]{0,1:T(8,128)}) %all-reduce.6.cloned.1.call-update) | async-done | bytes 262160 | tf_op jit(solution)/shard_map/psum | solution.py:46
  739.2 1.8 fusion.30
  (33 shorter events, 3.4 us)
Async XLA Ops:
  7.2 251.8 %all-reduce.4.cloned.1.call-start = ((), (), s32[]{:S(2)}) async-start(), calls=%async_computation | async-start | bytes 131072 | tf_op jit(solution)/shard_map/psum | solution.py:31
  8.9 621.6 %all-reduce.8.cloned.1.call-start = ((), (), s32[]{:S(2)}) async-start(), calls=%async_computation.2 | async-start | bytes 131072 | tf_op jit(solution)/shard_map/psum | solution.py:42
  31.4 227.6 %copy-start = (f32[12,128]{1,0:T(8,128)S(1)}, f32[12,128]{1,0:T(8,128)}, u32[]{:S(2)}) copy-start(f32[12,128]{1,0:T(8,128)} %param.8) | copy-start | bytes 18436
  46.9 213.3 %collective-permute-start = (f32[512,128]{0,1:T(8,128)S(1)}, f32[512,128]{0,1:T(8,128)S(1)}, u32[]{:S(2)}, u32[]{:S(2)}) collective-permute-start(f32[512,128]{0,1:T(8,128)S(1)} %fusion.8), channel_id=1, source_target_pairs={{0,1},{1,0},{2,3},{3,2},{4,5},{5,4},{6,7},{7,6},{8,9},{9,8},{10,11... | collective-permute-start | bytes 786440 | tf_op jit(solution)/shard_map/ppermute | solution.py:37
  260.3 13.5 %collective-permute-start.1 = (f32[512,128]{0,1:T(8,128)S(1)}, f32[512,128]{0,1:T(8,128)S(1)}, u32[]{:S(2)}, u32[]{:S(2)}) collective-permute-start(f32[512,128]{0,1:T(8,128)S(1)} %add.43), channel_id=1, source_target_pairs={{0,2},{1,3},{2,0},{3,1},{4,6},{5,7},{6,4},{7,5},{8,10},{9,11},{10,... | collective-permute-start | bytes 786440 | tf_op jit(solution)/shard_map/ppermute | solution.py:37
  273.8 12.9 %collective-permute-start.2 = (f32[512,128]{0,1:T(8,128)S(1)}, f32[512,128]{0,1:T(8,128)S(1)}, u32[]{:S(2)}, u32[]{:S(2)}) collective-permute-start(f32[512,128]{0,1:T(8,128)S(1)} %add.44), channel_id=1, source_target_pairs={{0,4},{1,5},{2,6},{3,7},{4,0},{5,1},{6,2},{7,3},{8,12},{9,13},{10,... | collective-permute-start | bytes 786440 | tf_op jit(solution)/shard_map/ppermute | solution.py:37
  286.7 9.3 %collective-permute-start.3 = (f32[512,128]{0,1:T(8,128)S(1)}, f32[512,128]{0,1:T(8,128)S(1)}, u32[]{:S(2)}, u32[]{:S(2)}) collective-permute-start(f32[512,128]{0,1:T(8,128)S(1)} %add.45), channel_id=1, source_target_pairs={{0,8},{1,9},{2,10},{3,11},{4,12},{5,13},{6,14},{7,15},{8,0},{9,1},... | collective-permute-start | bytes 786440 | tf_op jit(solution)/shard_map/ppermute | solution.py:37
  296.4 102.1 %copy-start.1 = (f32[32,128]{1,0:T(8,128)}, f32[32,128]{1,0:T(8,128)S(1)}, u32[]{:S(2)}) copy-start(f32[32,128]{1,0:T(8,128)S(1)} %get-tuple-element.7) | copy-start | bytes 49156
  387.9 351.2 %all-reduce.6.cloned.1.call-start = ((), (), s32[]{:S(2)}) async-start(), calls=%async_computation.1 | async-start | bytes 524288 | tf_op jit(solution)/shard_map/psum | solution.py:46
Sparse Core Ops, SparseCore 0:
  13.5 245.4 all-reduce.3
  388.1 242.4 all-reduce.7
  632.9 106.2 all-reduce.5
